TPU v7x, 32 devices: a whole 2x2x4 slice. The times are simulated.
32 devices in a mesh: groups: 2 (over y), tensor: 4 (over z), query: 2 (over x), dp: 2 (over core).
Axes of the slice: x: 2, y: 2, z: 4, core: 2. Of those that a mesh axis runs over, the one named last changes fastest.
Arguments:
- features: bfloat16 [2048, 8192], P(('groups', 'dp'), 'query'), parts along dimension 0, may hold values from -6 to 6
- up_weight: bfloat16 [8192, 28672], P(('query', 'dp'), 'tensor'), may hold values from -0.09375 to 0.09375
- out_grad: bfloat16 [2048, 28672], P(('groups', 'dp'), 'tensor'), parts along dimension 0, may hold values from -6 to 6
- left_factors: bfloat16 [16, 32, 28672], P('query', None, 'tensor'), may hold values from -0.03125 to 0.03125
- right_factors: bfloat16 [16, 32, 8192], P('query', None, 'tensor'), may hold values from -0.0625 to 0.0625
- token_ids: int32 [2048], P(('groups', 'dp')), parts along dimension 0, may hold values from 0 to 15, never falling along the last dimension, each value on 1 to 128 neighbouring positions
- query_ids: int32 [2, 8], P('query'), may hold values from 0 to 7, each once within a row
Outputs:
- input_grad: bfloat16 [2048, 8192], P(('groups', 'dp'), ('query', 'tensor')), parts along dimension 0
- scores: float32 [32, 16], P('groups', 'query'), parts along dimension 0
There are 2 independent parts, one for each index of `groups`. A program takes and returns all parts, laid end to end along the dimension named above; an argument that names none is the same for every part. Nothing has to cross between parts.
Inputs may be any that keep to these rules, and one draw needn't show every extreme that they name: token_ids never fall along the tokens; every example has at least one token. `query_ids`: each row is a permutation of the numbers below 8.
All inputs are finite; a program needn't handle non-finite values.
Results may differ from a plain program's by a relative error of at most 0.0049.
Values may be sent and summed in bfloat16 or wider, within the bound.
A program may use at most 192 MiB of HBM per device.

v0:
```python
import jax
import jax.numpy as jnp
from jax import lax
from jax.sharding import PartitionSpec as P

EXAMPLES = 16


def broadcast(value, axis, source):
    kept = jnp.where(lax.axis_index(axis) == source, value, 0).astype(value.dtype)
    return lax.psum(kept, axis)


def silu_slope(preact, grad_part):
    sigmoid_value = jax.nn.sigmoid(preact)
    return (
        grad_part.astype(jnp.float32) * sigmoid_value * (1.0 + preact * (1.0 - sigmoid_value))
    ).astype(jnp.bfloat16)


def contract_last(left_rows, right_rows):
    return lax.dot_general(
        left_rows, right_rows, (((1,), (1,)), ((), ())), preferred_element_type=jnp.float32
    )


def local(features, up_weight, out_grad, left_factors, right_factors, token_ids, query_ids):
    query_count = left_factors.shape[0]
    rank_count = left_factors.shape[1]
    local_rows = lax.all_gather(up_weight, "dp", axis=0, tiled=True)
    preact_part = jnp.dot(features, local_rows, preferred_element_type=jnp.float32)
    preact_share = lax.psum_scatter(preact_part, "query", scatter_dimension=0, tiled=True)
    share_rows = preact_share.shape[0]
    own_grad = lax.dynamic_slice_in_dim(
        out_grad, lax.axis_index("query") * share_rows, share_rows, 0
    )
    grad_rows = lax.all_gather(silu_slope(preact_share, own_grad), "query", axis=0, tiled=True)
    input_part = contract_last(grad_rows, local_rows)
    input_grad = lax.psum_scatter(input_part, "tensor", scatter_dimension=1, tiled=True).astype(
        jnp.bfloat16
    )
    fold_ratio = lax.axis_size("tensor") // lax.axis_size("query")
    tensor_index = lax.axis_index("tensor")
    block_width = right_factors.shape[2]
    feature_piece = lax.dynamic_slice_in_dim(
        features, tensor_index % fold_ratio * block_width, block_width, 1
    )
    feature_block = broadcast(feature_piece, "query", tensor_index // fold_ratio)
    left_proj = contract_last(
        grad_rows, left_factors.reshape(query_count * rank_count, left_factors.shape[2])
    )
    right_proj = contract_last(
        feature_block, right_factors.reshape(query_count * rank_count, block_width)
    )
    column_order = (
        query_ids[0][:, None] == jnp.arange(query_count, dtype=jnp.int32)[None, :]
    ).astype(jnp.float32)
    left_sum, right_sum = lax.psum((left_proj, right_proj), "tensor")
    per_token = (left_sum * right_sum).reshape(-1, query_count, rank_count).sum(axis=-1)
    membership = (token_ids[None, :] == jnp.arange(EXAMPLES, dtype=jnp.int32)[:, None]).astype(
        jnp.float32
    )
    summed = jnp.dot(
        membership, per_token, precision=lax.Precision.HIGHEST, preferred_element_type=jnp.float32
    )
    ordered = lax.dot_general(
        summed,
        column_order,
        (((1,), (1,)), ((), ())),
        precision=lax.Precision.HIGHEST,
        preferred_element_type=jnp.float32,
    )
    scores = lax.psum(ordered / rank_count, "dp")
    return (input_grad, scores)


def solution(mesh):
    return jax.shard_map(
        local,
        mesh=mesh,
        in_specs=(
            P(("groups", "dp"), "query"),
            P(("query", "dp"), "tensor"),
            P(("groups", "dp"), "tensor"),
            P("query", None, "tensor"),
            P("query", None, "tensor"),
            P(("groups", "dp")),
            P("query", None),
        ),
        out_specs=(P(("groups", "dp"), ("query", "tensor")), P("groups", "query")),
        check_vma=False,
    )
```

profile of v0, /device:TPU:0, one launch (start us, length us, event | category | flops | bytes accessed | tf_op | source)
XLA Modules:
  0.0 677.9 jit_solution(4646271791515592685)
XLA Ops:
  7.2 0.0 copy-start
  7.2 0.0 all-gather.3.cloned.1.call-start
  7.2 0.7 all-gather.3.cloned.1.call-update
  7.9 0.0 reduce-scatter.3.cloned.1.call-start
  8.0 88.3 %all-gather.3.cloned.1.call-done = bf16[4096,7168]{1,0:T(8,128)(2,1)} async-done(((bf16[2048,7168]{1,0:T(8,128)(2,1)}), bf16[4096,7168]{1,0:T(8,128)(2,1)}) %all-gather.3.cloned.1.call-update) | async-done | bytes 58720272 | tf_op jit(solution)/shard_map/all_gather | solution.py:30
  96.2 39.5 %fusion.3 = f32[512,7168]{1,0:T(8,128)} fusion(bf16[512,4096]{1,0:T(8,128)(2,1)} %param.7, bf16[4096,7168]{1,0:T(8,128)(2,1)} %all-gather.3.cloned.1.call-done), kind=kOutput, calls=%fused_computation.9 | convolution fusion | flops 30064771072 | bytes 77594624 | tf_op jit(solution)/shard_map/dot_general | solution.py:31
  135.7 0.0 reduce-scatter.3.cloned.1.call-update
  135.7 0.0 all-reduce.4.cloned.1.call-start
  135.8 3.5 dynamic-slice_select_fusion
  139.3 0.0 all-reduce.4.cloned.1.call-update
  139.3 0.0 all-gather.5.cloned.1.call-start
  139.3 164.9 %reduce-scatter.3.cloned.1.call-done = f32[256,7168]{1,0:T(8,128)} async-done(((f32[512,7168]{1,0:T(8,128)}), f32[256,7168]{1,0:T(8,128)}) %reduce-scatter.3.cloned.1.call-update) | async-done | bytes 7340048 | tf_op jit(solution)/shard_map/reduce_scatter | solution.py:32
  304.2 6.8 multiply_convert_fusion
  311.0 0.0 all-gather.5.cloned.1.call-update
  311.0 0.0 all-reduce.6.cloned.1.call-start
  311.0 58.5 %all-reduce.4.cloned.1.call-done = bf16[512,2048]{1,0:T(8,128)(2,1)} async-done(((bf16[512,2048]{1,0:T(8,128)(2,1)}), bf16[512,2048]{1,0:T(8,128)(2,1)}) %all-reduce.4.cloned.1.call-update) | async-done | bytes 2097168 | tf_op jit(solution)/shard_map/psum | solution.py:11
  369.5 0.0 copy-done
  369.5 3.1 fusion.6
  372.6 90.5 %all-gather.5.cloned.1.call-done = bf16[512,7168]{1,0:T(8,128)(2,1)} async-done(((bf16[256,7168]{1,0:T(8,128)(2,1)}), bf16[512,7168]{1,0:T(8,128)(2,1)}) %all-gather.5.cloned.1.call-update) | async-done | bytes 7340048 | tf_op jit(solution)/shard_map/all_gather | solution.py:37
  463.1 7.0 %fusion.5 = f32[512,256]{1,0:T(8,128)} fusion(bf16[512,7168]{1,0:T(8,128)(2,1)} %all-gather.5.cloned.1.call-done, bf16[256,7168]{1,0:T(8,128)(2,1)} %bitcast.16), kind=kOutput, calls=%fused_computation.11 | convolution fusion | flops 1879048192 | bytes 11534336 | tf_op jit(solution)/shard_map/dot_general | solution.py:22
  470.1 0.0 all-reduce.6.cloned.1.call-update
  470.1 0.2 reduce-scatter.5.cloned.1.call-start
  470.4 38.9 %fusion.4 = f32[512,4096]{1,0:T(8,128)} fusion(bf16[512,7168]{1,0:T(8,128)(2,1)} %all-gather.5.cloned.1.call-done, bf16[4096,7168]{1,0:T(8,128)(2,1)} %all-gather.3.cloned.1.call-done), kind=kOutput, calls=%fused_computation.10 | convolution fusion | flops 30064771072 | bytes 74448896 | tf_op jit(solution)/shard_map/dot_general | solution.py:22
  509.3 0.0 copy-start.2
  509.3 0.0 copy-start.3
  509.3 0.0 copy-start.1
  509.3 0.0 reduce-scatter.5.cloned.1.call-update
  509.3 13.0 %all-reduce.6.cloned.1.call-done = (f32[512,256]{1,0:T(8,128)}, f32[512,256]{1,0:T(8,128)}) async-done(((f32[512,256]{1,0:T(8,128)}, f32[512,256]{1,0:T(8,128)}), (f32[512,256]{1,0:T(8,128)}, f32[512,256]{1,0:T(8,128)})) %all-reduce.6.cloned.1.call-update) | async-done | bytes 1048592 | tf_op jit(solution)/shard_map/psum | solution.py:58
  522.2 1.3 mul.23
  523.5 0.2 copy.10
  523.7 0.1 bitcast_reduce_fusion
  523.8 0.0 copy-done.2
  523.8 0.1 fusion
  523.9 0.0 copy-done.3
  523.9 0.2 convolution_multiply_fusion
  524.1 3.0 psum.31
  527.2 141.2 %reduce-scatter.5.cloned.1.call-done = f32[512,1024]{1,0:T(8,128)} async-done(((f32[512,4096]{1,0:T(8,128)}), f32[512,1024]{1,0:T(8,128)}) %reduce-scatter.5.cloned.1.call-update) | async-done | bytes 2097168 | tf_op jit(solution)/shard_map/reduce_scatter | solution.py:39
  668.4 2.7 convert_element_type.15
  671.1 0.0 copy-done.1
Async XLA Ops:
  7.2 362.3 %copy-start = (bf16[8,32,2048]{2,1,0:T(8,128)(2,1)S(1)}, bf16[8,32,2048]{2,1,0:T(8,128)(2,1)}, u32[]{:S(2)}) copy-start(bf16[8,32,2048]{2,1,0:T(8,128)(2,1)} %param.11) | copy-start | bytes 3145732
  7.2 89.0 %all-gather.3.cloned.1.call-start = ((), (), s32[]{:S(2)}) async-start(), calls=%async_computation.2 | async-start | bytes 88080384 | tf_op jit(solution)/shard_map/all_gather | solution.py:30
  7.9 296.3 %reduce-scatter.3.cloned.1.call-start = ((), (), s32[]{:S(2)}) async-start(), calls=%async_computation.3 | async-start | bytes 22020096 | tf_op jit(solution)/shard_map/reduce_scatter | solution.py:32
  135.7 233.8 %all-reduce.4.cloned.1.call-start = ((), (), s32[]{:S(2)}) async-start(), calls=%async_computation.6 | async-start | bytes 4194304 | tf_op jit(solution)/shard_map/psum | solution.py:11
  139.3 323.8 %all-gather.5.cloned.1.call-start = ((), (), s32[]{:S(2)}) async-start(), calls=%async_computation.4 | async-start | bytes 11010048 | tf_op jit(solution)/shard_map/all_gather | solution.py:37
  311.0 211.3 %all-reduce.6.cloned.1.call-start = ((), (), s32[]{:S(2)}) async-start(), calls=%async_computation.7 | async-start | bytes 2097152 | tf_op jit(solution)/shard_map/psum | solution.py:58
  470.1 198.2 %reduce-scatter.5.cloned.1.call-start = ((), (), s32[]{:S(2)}) async-start(), calls=%async_computation.5 | async-start | bytes 10485760 | tf_op jit(solution)/shard_map/reduce_scatter | solution.py:39
  509.3 14.5 %copy-start.2 = (s32[512]{0:T(512)S(1)}, s32[512]{0:T(512)}, u32[]{:S(2)}) copy-start(s32[512]{0:T(512)} %param.12) | copy-start | bytes 6148
  509.3 14.7 %copy-start.3 = (s32[1,8]{1,0:T(1,128)S(1)}, s32[1,8]{1,0:T(1,128)}, u32[]{:S(2)}) copy-start(s32[1,8]{1,0:T(1,128)} %param.13) | copy-start | bytes 100
  509.3 161.8 %copy-start.1 = (bf16[8,32,2048]{2,1,0:T(8,128)(2,1)S(1)}, bf16[8,32,2048]{2,1,0:T(8,128)(2,1)}, u32[]{:S(2)}) copy-start(bf16[8,32,2048]{2,1,0:T(8,128)(2,1)} %param.11) | copy-start | bytes 3145732
Sparse Core Ops, SparseCore 0:
  9.5 86.6 all-gather.2
  135.8 168.3 reduce-scatter.2
  306.5 62.9 all-reduce.3
  370.9 92.1 all-gather.4
  470.3 51.9 all-reduce.5
  524.5 143.8 reduce-scatter.4
where the time goes:
time: 678 us
  waiting for transfers between devices  557 us (82%)
  matrix products  88.8 us (13%)
  other arithmetic  14.3 us (2%)
  between operations  14.2 us (2%)
    reduce_scatter x1, waiting for transfers between devices, local(): lax.psum_scatter(preact_part, 'query', scatter_dimension=0, tiled=True)  165 us
    reduce_scatter x1, waiting for transfers between devices, local(): lax.psum_scatter(input_part, 'tensor', scatter_dimension=1, tiled=True)  141 us
    all_gather x1, waiting for transfers between devices, local(): lax.all_gather(silu_slope(preact_share, own_grad), 'query', axis=0, tiled...  90.5 us
    all_gather x1, waiting for transfers between devices, local(): local_rows = lax.all_gather(up_weight, 'dp', axis=0, tiled=True)  88.3 us
    psum x1, waiting for transfers between devices, broadcast(): return lax.psum(kept, axis)  58.5 us
    dot_general x3, matrix products, contract_last(): lax.dot_general(left_rows, right_rows, (((1,), (1,)), ((), ())), preferre...  49 us
    dot_general x1, matrix products, local(): jnp.dot(features, local_rows, preferred_element_type=jnp.float32)  39.5 us
  transfers between devices with their start and end apart: 6, of which 6 were waited for; matrix products, arithmetic and copies ran while one was open for 8% of the time, Pallas kernels for 0%

commit v1 on v0

v1 whole, which is shorter than its diff:
```python
import jax
import jax.numpy as jnp
from jax import lax
from jax.sharding import PartitionSpec as P


EXAMPLES = 16
CHUNKS = 4


def shifted(value, axis, step):
    size = lax.axis_size(axis)
    return lax.ppermute(value, axis, [(i, (i + step) % size) for i in range(size)])


def contract_last(left_rows, right_rows, out_type=jnp.float32):
    return lax.dot_general(
        left_rows, right_rows, (((1,), (1,)), ((), ())), preferred_element_type=jnp.float32
    ).astype(out_type)


def silu_slope(preact, grad_part):
    sigmoid_value = jax.nn.sigmoid(preact)
    return (
        grad_part.astype(jnp.float32) * sigmoid_value * (1.0 + preact * (1.0 - sigmoid_value))
    ).astype(jnp.bfloat16)


def total_over(value, axis):
    parts = [shifted(value, axis, step) for step in range(1, lax.axis_size(axis))]
    for part in parts:
        value = value + part
    return value


def right_parts(features, right_factors, gate):
    queries, tensors = lax.axis_size("query"), lax.axis_size("tensor")
    query_index, tensor_index = lax.axis_index("query"), lax.axis_index("tensor")
    fold = tensors // queries
    width = right_factors.shape[2]
    flat = right_factors.reshape(-1, width)
    piece = lax.dynamic_slice_in_dim(features, tensor_index % fold * width, width, 1)
    rows = piece.shape[0] // tensors
    holder = (tensor_index // fold == query_index).astype(jnp.float32)
    moved = [shifted(flat, "query", step) for step in range(1, queries)]
    factors = [flat] + moved
    factors, _ = lax.optimization_barrier((factors, gate))
    part = contract_last(piece, jnp.concatenate(factors, axis=0)) * holder
    block = lax.dynamic_slice_in_dim(part, tensor_index * rows, rows, 0)
    for hop in range(1, tensors):
        send = lax.dynamic_slice_in_dim(part, (tensor_index + hop) % tensors * rows, rows, 0)
        moved = shifted(send, "tensor", hop)
        block = block + moved
    return jnp.split(block, queries, axis=1)


def right_whole(total):
    tensors, tensor_index = lax.axis_size("tensor"), lax.axis_index("tensor")
    rows = total.shape[0]
    others = [shifted(total, "tensor", hop) for hop in range(1, tensors)]
    turned = (others[::-1] + [total]) * 2
    return lax.dynamic_slice_in_dim(
        jnp.concatenate(turned, axis=0), (tensors - 1 - tensor_index) * rows, tensors * rows, 0
    )


def scatter_blocks(input_part, rows):
    tensors, cores = lax.axis_size("tensor"), lax.axis_size("dp")
    tensor_index, core = lax.axis_index("tensor"), lax.axis_index("dp")
    per_core = tensors // cores
    width = input_part.shape[1] // per_core
    parts = []
    for step in range(tensors):
        pick = (tensor_index + step) % tensors
        block = lax.dynamic_slice(
            input_part,
            ((core - pick % cores) % cores * rows, pick // cores * width),
            (rows, width),
        )
        perm = []
        for t in range(tensors):
            for d in range(cores):
                k = (t + step) % tensors
                perm.append((t * cores + d, (d * per_core + k // cores) * cores + k % cores))
        parts.append(lax.ppermute(block, ("tensor", "dp"), perm))
    return parts


def add_blocks(parts):
    total = parts[0].astype(jnp.float32)
    for part in parts[1:]:
        total = total + part.astype(jnp.float32)
    return total.astype(jnp.bfloat16)


def local(features, up_weight, out_grad, left_factors, right_factors, token_ids, query_ids):
    query_count, rank_count = left_factors.shape[0], left_factors.shape[1]
    cores, queries = lax.axis_size("dp"), lax.axis_size("query")
    core = lax.axis_index("dp")
    depth = up_weight.shape[0]
    tokens = features.shape[0]
    rows = tokens // CHUNKS
    flat_left = left_factors.reshape(query_count * rank_count, left_factors.shape[2])

    sets = [lax.dynamic_slice_in_dim(features, core * depth, depth, 1)]
    for step in range(1, cores):
        piece = lax.dynamic_slice_in_dim(features, (core + step) % cores * depth, depth, 1)
        sets.append(shifted(piece, "dp", step))

    sums, received, backs = [], [], []
    partials, sends = [], []
    for c in range(CHUNKS):
        span = slice(c * rows, (c + 1) * rows)
        stacked = jnp.concatenate([part[span] for part in sets], axis=0)
        partial = jnp.dot(stacked, up_weight, preferred_element_type=jnp.float32).astype(
            jnp.bfloat16
        )
        partials.append(partial)
        pieces = [partial[step * rows : (step + 1) * rows] for step in range(1, cores)]
        backs.append([shifted(piece, "dp", cores - i - 1) for i, piece in enumerate(pieces)])
    for c in range(CHUNKS):
        if c + 1 < CHUNKS:
            backs[c], _ = lax.optimization_barrier((backs[c], partials[c + 1]))
        own = partials[c][:rows].astype(jnp.float32)
        for back in backs[c]:
            own = own + back.astype(jnp.float32)
        send = own.astype(jnp.bfloat16)
        sends.append(send)
        if c == CHUNKS - 1:
            blocks = right_parts(features, right_factors, received_gate)
            send, blocks = lax.optimization_barrier((send, blocks))
            right_total = blocks[0]
            for step in range(1, queries):
                moved = shifted(blocks[step], "query", queries - step)
                right_total = right_total + moved
        sums.append(own)
        received.append([shifted(send, "query", step) for step in range(1, queries)])
        received_gate = send

    outputs, projections = [], []
    gate, waiting = (partials[-1], sends), None
    for c in range(CHUNKS):
        span = slice(c * rows, (c + 1) * rows)
        parts, _ = lax.optimization_barrier((received[c], gate))
        preact = sums[c]
        for part in parts:
            preact = preact + part.astype(jnp.float32)
        grad_rows = silu_slope(preact, out_grad[span])
        others = [shifted(grad_rows, "dp", step) for step in range(1, cores)]
        stacked = jnp.concatenate([grad_rows] + others, axis=0)
        input_part = contract_last(stacked, up_weight, jnp.bfloat16)
        if waiting is not None:
            waiting, _ = lax.optimization_barrier((waiting, input_part))
            outputs.append(add_blocks(waiting))
        waiting = scatter_blocks(input_part, rows)
        gate = input_part
        projections.append(contract_last(grad_rows, flat_left))
    right_sum = right_whole(right_total)
    outputs.append(add_blocks(waiting))
    input_grad = jnp.concatenate(outputs, axis=0)

    left_part = jnp.concatenate(projections, axis=0)
    per_token = (left_part * right_sum).reshape(-1, query_count, rank_count).sum(axis=-1)
    membership = (token_ids[None, :] == jnp.arange(EXAMPLES, dtype=jnp.int32)[:, None]).astype(
        jnp.float32
    )
    summed = jnp.dot(
        membership, per_token, precision=lax.Precision.HIGHEST, preferred_element_type=jnp.float32
    )
    column_order = (
        query_ids[0][:, None] == jnp.arange(query_count, dtype=jnp.int32)[None, :]
    ).astype(jnp.float32)
    ordered = lax.dot_general(
        summed,
        column_order,
        (((1,), (1,)), ((), ())),
        precision=lax.Precision.HIGHEST,
        preferred_element_type=jnp.float32,
    )
    scores = total_over(ordered / rank_count, "dp")
    scores, _ = lax.optimization_barrier((scores, input_part))
    scores = total_over(scores, "tensor")
    return (input_grad, scores)


def solution(mesh):
    return jax.shard_map(
        local,
        mesh=mesh,
        in_specs=(
            P(("groups", "dp"), "query"),
            P(("query", "dp"), "tensor"),
            P(("groups", "dp"), "tensor"),
            P("query", None, "tensor"),
            P("query", None, "tensor"),
            P(("groups", "dp")),
            P("query", None),
        ),
        out_specs=(P(("groups", "dp"), ("query", "tensor")), P("groups", "query")),
        check_vma=False,
    )
```

time: 678 us -> 401 us (0.59)
  waiting for transfers between devices: 557 us -> 157 us
  starting transfers between devices: 0.42 us -> 67.5 us
  matrix products: 88.8 us -> 126 us
  other arithmetic: 14.3 us -> 30 us
  local copies, waits for them, and re-layouts: 0.22 us -> 15.7 us
  between operations: 14.2 us -> 1.43 us
    reduce_scatter x2 -> x0, waiting for transfers between devices: 306 us -> none  [the longest x1 165 us: local(): lax.psum_scatter(preact_part, 'query', scatter_dimension=0, tiled=True)]
    all_gather x2 -> x0, waiting for transfers between devices: 179 us -> none  [the longest x1 90.5 us: local(): lax.all_gather(silu_slope(preact_share, own_grad), 'query', axis=0, tiled...]
    ppermute x0 -> x41, waiting for transfers between devices: none -> 157 us  [the longest x25 128 us: shifted(): lax.ppermute(value, axis, [(i, (i + step) % size) for i in range(size)])]
    psum x2 -> x0, waiting for transfers between devices: 71.4 us -> none  [the longest x1 58.5 us: broadcast(): return lax.psum(kept, axis)]
    ppermute x0 -> x41, starting transfers between devices: none -> 67.5 us  [the longest x16 35.2 us: scatter_blocks(): parts.append(lax.ppermute(block, ('tensor', 'dp'), perm))]
    dot_general x3 -> x9, matrix products: 49 us -> 72.2 us  [contract_last(): lax.dot_general(left_rows, right_rows, (((1,), (1,)), ((), ())), preferre...]
    dot_general x1 -> x4, matrix products: 39.5 us -> 53.8 us  [local(): jnp.dot(stacked, up_weight, preferred_element_type=jnp.float32)]
    convert_element_type x1 -> x7, other arithmetic: 2.72 us -> 12.2 us  [the longest x4 10.5 us: local(): send = own.astype(jnp.bfloat16)]
  transfers between devices with their start and end apart: 6 -> 41, of which waited for: 6 -> 13; matrix products, arithmetic and copies ran while one was open for 8% -> 37% of each run, Pallas kernels for 0% -> 0%
where the time goes in v1:
time: 401 us; the launch traced here: 398 us
  waiting for transfers between devices  157 us (39%)
  matrix products  126 us (31%)
  starting transfers between devices  67.5 us (17%)
  other arithmetic  30 us (7%)
  local copies, waits for them, and re-layouts  15.7 us (4%)
    ppermute x25, waiting for transfers between devices, shifted(): lax.ppermute(value, axis, [(i, (i + step) % size) for i in range(size)])  128 us
    dot_general x9, matrix products, contract_last(): lax.dot_general(left_rows, right_rows, (((1,), (1,)), ((), ())), preferre...  72.2 us
    dot_general x4, matrix products, local(): jnp.dot(stacked, up_weight, preferred_element_type=jnp.float32)  53.8 us
    ppermute x16, starting transfers between devices, scatter_blocks(): parts.append(lax.ppermute(block, ('tensor', 'dp'), perm))  35.2 us
    ppermute x25, starting transfers between devices, shifted(): lax.ppermute(value, axis, [(i, (i + step) % size) for i in range(size)])  32.3 us
    ppermute x16, waiting for transfers between devices, scatter_blocks(): parts.append(lax.ppermute(block, ('tensor', 'dp'), perm))  29.1 us
    convert_element_type x4, other arithmetic, silu_slope(): return (grad_part.astype(jnp.float32) * sigmoid_value * (1.0 + preact * (...  15.9 us
    convert_element_type x4, other arithmetic, local(): send = own.astype(jnp.bfloat16)  10.5 us
  transfers between devices with their start and end apart: 41, of which 13 were waited for; matrix products, arithmetic and copies ran while one was open for 37% of the time, Pallas kernels for 0%

profile of v1, /device:TPU:0, one launch (start us, length us, event | category | flops | bytes accessed | tf_op | source)
XLA Modules:
  0.0 398.4 jit_solution(9712440017466615730)
XLA Ops:
  0.6 3.2 constant_dynamic-slice_fusion.4
  4.3 1.7 constant_dynamic-slice_fusion
  6.0 2.3 collective-permute-done
  8.3 1.1 fusion.67
  9.4 13.3 %convolution_convert_fusion = bf16[256,7168]{1,0:T(8,128)(2,1)S(1)} fusion(bf16[2048,7168]{1,0:T(8,128)(2,1)} %param.8, bf16[128,2048]{1,0:T(8,128)(2,1)S(1)} %get-tuple-element.57, bf16[128,2048]{1,0:T(8,128)(2,1)S(1)} %get-tuple-element.55), kind=kOutput, calls=%fused_computation | convolution fusion | flops 7520124928 | bytes 34078720 | tf_op jit(solution)/shard_map/dot_general | solution.py:115
  22.7 1.5 slice.89
  24.6 13.3 %convolution_convert_fusion.1 = bf16[256,7168]{1,0:T(8,128)(2,1)S(1)} fusion(bf16[2048,7168]{1,0:T(8,128)(2,1)} %param.8, bf16[128,2048]{1,0:T(8,128)(2,1)S(1)} %get-tuple-element.58, bf16[128,2048]{1,0:T(8,128)(2,1)S(1)} %get-tuple-element.53), kind=kOutput, calls=%fused_computation.1 | convolution fusion | flops 7520124928 | bytes 34078720 | tf_op jit(solution)/shard_map/dot_general | solution.py:115
  37.9 1.4 slice.91
  39.7 13.5 %convolution_convert_fusion.3 = bf16[256,7168]{1,0:T(8,128)(2,1)S(1)} fusion(bf16[2048,7168]{1,0:T(8,128)(2,1)} %param.8, bf16[128,2048]{1,0:T(8,128)(2,1)S(1)} %copy-done.16, bf16[128,2048]{1,0:T(8,128)(2,1)S(1)} %get-tuple-element.52), kind=kOutput, calls=%fused_computation.3 | convolution fusion | flops 7520124928 | bytes 34078720 | tf_op jit(solution)/shard_map/dot_general | solution.py:115
  53.3 1.5 slice.82
  55.7 13.6 %convolution_convert_fusion.2 = bf16[256,7168]{1,0:T(8,128)(2,1)S(1)} fusion(bf16[2048,7168]{1,0:T(8,128)(2,1)} %param.8, bf16[128,2048]{1,0:T(8,128)(2,1)} %get-tuple-element.59, bf16[128,2048]{1,0:T(8,128)(2,1)S(1)} %get-tuple-element.54), kind=kOutput, calls=%fused_computation.2 | convolution fusion | flops 7520124928 | bytes 34078720 | tf_op jit(solution)/shard_map/dot_general | solution.py:115
  69.9 3.5 fusion.18
  73.4 1.9 fusion.16
  75.4 2.5 collective-permute-start.2
  77.9 1.8 fusion.17
  79.7 3.2 fusion.19
  82.9 35.7 %collective-permute-done.2 = bf16[128,7168]{1,0:T(8,128)(2,1)S(1)} collective-permute-done((bf16[128,7168]{1,0:T(8,128)(2,1)S(1)}, bf16[128,7168]{1,0:T(8,128)(2,1)S(1)}, u32[]{:S(2)}, u32[]{:S(2)}) %collective-permute-start.2) | collective-permute-done | bytes 1835040 | tf_op jit(solution)/shard_map/ppermute | solution.py:13
  118.6 3.3 multiply_convert_fusion.3
  122.1 1.8 collective-permute-start.23
  124.1 1.8 collective-permute-done.6
  125.9 15.0 %fusion.29 = bf16[256,2048]{1,0:T(8,128)(2,1)} fusion(bf16[2048,7168]{1,0:T(8,128)(2,1)} %param.8, bf16[128,7168]{1,0:T(8,128)(2,1)} %collective-permute-done.6, bf16[128,7168]{1,0:T(8,128)(2,1)S(1)} %multiply_convert_fusion.3), kind=kOutput, calls=%fused_computation.35 | convolution fusion | flops 7524057088 | bytes 34078720 | tf_op jit(solution)/shard_map/dot_general | solution.py:17
  140.9 46.3 %collective-permute-done.11 = bf16[128,7168]{1,0:T(8,128)(2,1)} collective-permute-done((bf16[128,7168]{1,0:T(8,128)(2,1)}, bf16[128,7168]{1,0:T(8,128)(2,1)}, u32[]{:S(2)}, u32[]{:S(2)}) %collective-permute-start.11) | collective-permute-done | bytes 1835040 | tf_op jit(solution)/shard_map/ppermute | solution.py:13
  187.3 4.2 %multiply_convert_fusion.2 = bf16[128,7168]{1,0:T(8,128)(2,1)} fusion(bf16[128,7168]{1,0:T(8,128)(2,1)} %collective-permute-done.11, bf16[128,7168]{1,0:T(8,128)(2,1)S(1)} %copy-done.12, bf16[512,7168]{1,0:T(8,128)(2,1)} %param.9, bf16[256,7168]{1,0:T(8,128)(2,1)S(1)} %convolution_convert_fusion.2), kind=kLoop, calls=%fused_computation.22 | loop fusion | flops 13762560 | bytes 9175040 | tf_op jit(solution)/shard_map/convert_element_type | solution.py:26
  191.5 3.5 fusion.49
  195.1 1.9 collective-permute-start.24
  196.9 2.6 collective-permute-start.25
  199.5 1.3 collective-permute-start.26
  200.9 5.4 %collective-permute-done.24 = f32[128,512]{1,0:T(8,128)S(1)} collective-permute-done((f32[128,512]{1,0:T(8,128)S(1)}, f32[128,512]{1,0:T(8,128)S(1)}, u32[]{:S(2)}, u32[]{:S(2)}) %collective-permute-start.24) | collective-permute-done | bytes 262176 | tf_op jit(solution)/shard_map/ppermute | solution.py:13
  206.3 11.0 %collective-permute-done.25 = f32[128,512]{1,0:T(8,128)S(1)} collective-permute-done((f32[128,512]{1,0:T(8,128)S(1)}, f32[128,512]{1,0:T(8,128)S(1)}, u32[]{:S(2)}, u32[]{:S(2)}) %collective-permute-start.25) | collective-permute-done | bytes 262176 | tf_op jit(solution)/shard_map/ppermute | solution.py:13
  217.4 1.6 collective-permute-start.33
  219.0 3.9 collective-permute-done.33
  222.9 6.9 %collective-permute-start.34 = (f32[128,256]{1,0:T(8,128)S(1)}, f32[128,256]{1,0:T(8,128)S(1)}, u32[]{:S(2)}, u32[]{:S(2)}) collective-permute-start(f32[128,256]{1,0:T(8,128)S(1)} %add.355), channel_id=1, source_target_pairs={{0,12},{4,0},{8,4},{12,8},{1,13},{5,1},{9,5},{13,9},{2,14},{6,2},{... | collective-permute-start | bytes 393224 | tf_op jit(solution)/shard_map/ppermute | solution.py:13
  229.7 1.5 collective-permute-start.17
  232.1 1.6 collective-permute-done.34
  234.3 15.7 %fusion.26 = bf16[256,2048]{1,0:T(8,128)(2,1)} fusion(bf16[2048,7168]{1,0:T(8,128)(2,1)} %param.8, bf16[128,7168]{1,0:T(8,128)(2,1)} %collective-permute-done.12, bf16[128,7168]{1,0:T(8,128)(2,1)} %multiply_convert_fusion.2), kind=kOutput, calls=%fused_computation.34 | convolution fusion | flops 7524057088 | bytes 34078720 | tf_op jit(solution)/shard_map/dot_general | solution.py:17
  250.0 20.4 %collective-permute-done.17 = bf16[128,7168]{1,0:T(8,128)(2,1)} collective-permute-done((bf16[128,7168]{1,0:T(8,128)(2,1)}, bf16[128,7168]{1,0:T(8,128)(2,1)}, u32[]{:S(2)}, u32[]{:S(2)}) %collective-permute-start.17) | collective-permute-done | bytes 1835040 | tf_op jit(solution)/shard_map/ppermute | solution.py:13
  270.5 3.6 multiply_convert_fusion.1
  275.3 1.4 fusion.73
  276.8 2.5 collective-permute-start.10
  280.0 5.8 %collective-permute-start.8 = (bf16[128,1024]{1,0:T(8,128)(2,1)S(1)}, bf16[128,1024]{1,0:T(8,128)(2,1)S(1)}, u32[]{:S(2)}, u32[]{:S(2)}) collective-permute-start(bf16[128,1024]{1,0:T(8,128)(2,1)S(1)} %get-tuple-element.62), channel_id=1, source_target_pairs={{0,1},{1,9},{4,4},{5,12},{8,5},{9,13},{12,0},{13,8},{2,3},{3,11},{... | collective-permute-start | bytes 786440 | tf_op jit(solution)/shard_map/ppermute | solution.py:85
  285.9 2.8 fusion.74
  288.8 1.6 collective-permute-start.27
  290.4 4.7 %collective-permute-done.8 = bf16[128,1024]{1,0:T(8,128)(2,1)S(1)} collective-permute-done((bf16[128,1024]{1,0:T(8,128)(2,1)S(1)}, bf16[128,1024]{1,0:T(8,128)(2,1)S(1)}, u32[]{:S(2)}, u32[]{:S(2)}) %collective-permute-start.8) | collective-permute-done | bytes 262176 | tf_op jit(solution)/shard_map/ppermute | solution.py:85
  295.0 10.6 %collective-permute-done.9 = bf16[128,1024]{1,0:T(8,128)(2,1)S(1)} collective-permute-done((bf16[128,1024]{1,0:T(8,128)(2,1)S(1)}, bf16[128,1024]{1,0:T(8,128)(2,1)S(1)}, u32[]{:S(2)}, u32[]{:S(2)}) %collective-permute-start.9) | collective-permute-done | bytes 262176 | tf_op jit(solution)/shard_map/ppermute | solution.py:85
  305.6 1.1 fusion.69
  306.7 1.6 collective-permute-start.13
  308.3 1.9 collective-permute-start.14
  310.4 1.3 copy-done.29
  311.6 3.5 collective-permute-start.16
  315.1 15.2 %fusion.23 = bf16[256,2048]{1,0:T(8,128)(2,1)} fusion(bf16[2048,7168]{1,0:T(8,128)(2,1)} %param.8, bf16[128,7168]{1,0:T(8,128)(2,1)} %copy-done.29, bf16[128,7168]{1,0:T(8,128)(2,1)} %copy-done.9), kind=kOutput, calls=%fused_computation.33 | convolution fusion | flops 7524057088 | bytes 34078720 | tf_op jit(solution)/shard_map/dot_general | solution.py:17
  330.4 4.7 %multiply_convert_fusion = bf16[128,7168]{1,0:T(8,128)(2,1)} fusion(bf16[128,7168]{1,0:T(8,128)(2,1)} %collective-permute-done.27, bf16[128,7168]{1,0:T(8,128)(2,1)} %collective-permute-done.5, bf16[512,7168]{1,0:T(8,128)(2,1)} %param.9, bf16[256,7168]{1,0:T(8,128)(2,1)S(1)} %copy-done.2), kind=kLoop, calls=%fused_computation.20 | loop fusion | flops 13762560 | bytes 9175040 | tf_op jit(solution)/shard_map/convert_element_type | solution.py:26
  335.1 2.6 collective-permute-start.28
  337.9 1.3 fusion.75
  339.3 3.0 fusion.76
  343.9 6.3 %collective-permute-start.20 = (bf16[128,1024]{1,0:T(8,128)(2,1)S(1)}, bf16[128,1024]{1,0:T(8,128)(2,1)S(1)}, u32[]{:S(2)}, u32[]{:S(2)}) collective-permute-start(bf16[128,1024]{1,0:T(8,128)(2,1)S(1)} %get-tuple-element.70), channel_id=1, source_target_pairs={{0,1},{1,9},{4,4},{5,12},{8,5},{9,13},{12,0},{13,8},{2,3},{3,11},{... | collective-permute-start | bytes 786440 | tf_op jit(solution)/shard_map/ppermute | solution.py:85
  350.2 3.2 collective-permute-start.22
  353.5 14.3 %fusion.20 = bf16[256,2048]{1,0:T(8,128)(2,1)S(1)} fusion(bf16[2048,7168]{1,0:T(8,128)(2,1)} %param.8, bf16[128,7168]{1,0:T(8,128)(2,1)} %collective-permute-done.28, bf16[128,7168]{1,0:T(8,128)(2,1)} %multiply_convert_fusion), kind=kOutput, calls=%fused_computation.32 | convolution fusion | flops 7524057088 | bytes 34078720 | tf_op jit(solution)/shard_map/dot_general | solution.py:17
  368.9 1.8 collective-permute-start.39
  370.6 1.8 collective-permute-start.40
  373.2 4.6 %collective-permute-start.30 = (bf16[128,1024]{1,0:T(8,128)(2,1)S(1)}, bf16[128,1024]{1,0:T(8,128)(2,1)S(1)}, u32[]{:S(2)}, u32[]{:S(2)}) collective-permute-start(bf16[128,1024]{1,0:T(8,128)(2,1)S(1)} %get-tuple-element.75), channel_id=1, source_target_pairs={{0,1},{1,9},{4,4},{5,12},{8,5},{9,13},{12,0},{13,8},{2,3},{3,11},{... | collective-permute-start | bytes 786440 | tf_op jit(solution)/shard_map/ppermute | solution.py:85
  377.9 3.5 collective-permute-start.32
  381.4 1.4 add_convert_fusion.1
  383.4 3.0 collective-permute-done.30
  386.4 10.8 %collective-permute-done.31 = bf16[128,1024]{1,0:T(8,128)(2,1)S(1)} collective-permute-done((bf16[128,1024]{1,0:T(8,128)(2,1)S(1)}, bf16[128,1024]{1,0:T(8,128)(2,1)S(1)}, u32[]{:S(2)}, u32[]{:S(2)}) %collective-permute-start.31) | collective-permute-done | bytes 262176 | tf_op jit(solution)/shard_map/ppermute | solution.py:85
  (135 shorter events, 12.4 us)
Async XLA Ops:
  3.8 4.5 %collective-permute-start = (bf16[512,2048]{1,0:T(8,128)(2,1)}, bf16[512,2048]{1,0:T(8,128)(2,1)S(1)}, u32[]{:S(2)}, u32[]{:S(2)}) collective-permute-start(bf16[512,2048]{1,0:T(8,128)(2,1)} %constant_dynamic-slice_fusion.4), channel_id=1, source_target_pairs={{0,1},{1,0},{2,3},{3,2},{4,5},{5,4},{6,7},{7,6},{8,9},{9,8},{10,11... | collective-permute-start | bytes 6291464 | tf_op jit(solution)/shard_map/ppermute | solution.py:13
  22.7 47.2 %copy-start.3 = (bf16[256,7168]{1,0:T(8,128)(2,1)}, bf16[256,7168]{1,0:T(8,128)(2,1)S(1)}, u32[]{:S(2)}) copy-start(bf16[256,7168]{1,0:T(8,128)(2,1)S(1)} %convolution_convert_fusion) | copy-start | bytes 11010052
  24.2 45.8 %collective-permute-start.4 = (bf16[128,7168]{1,0:T(8,128)(2,1)}, bf16[128,7168]{1,0:T(8,128)(2,1)}, u32[]{:S(2)}, u32[]{:S(2)}) collective-permute-start(bf16[128,7168]{1,0:T(8,128)(2,1)} %slice.89), channel_id=1, source_target_pairs={{0,1},{1,0},{2,3},{3,2},{4,5},{5,4},{6,7},{7,6},{8,9},{9,8},{10,11... | collective-permute-start | bytes 5505032 | tf_op jit(solution)/shard_map/ppermute | solution.py:13
  37.9 41.8 %copy-start.1 = (bf16[256,7168]{1,0:T(8,128)(2,1)}, bf16[256,7168]{1,0:T(8,128)(2,1)S(1)}, u32[]{:S(2)}) copy-start(bf16[256,7168]{1,0:T(8,128)(2,1)S(1)} %convolution_convert_fusion.1) | copy-start | bytes 11010052
  39.3 40.4 %collective-permute-start.5 = (bf16[128,7168]{1,0:T(8,128)(2,1)}, bf16[128,7168]{1,0:T(8,128)(2,1)}, u32[]{:S(2)}, u32[]{:S(2)}) collective-permute-start(bf16[128,7168]{1,0:T(8,128)(2,1)} %slice.91), channel_id=1, source_target_pairs={{0,1},{1,0},{2,3},{3,2},{4,5},{5,4},{6,7},{7,6},{8,9},{9,8},{10,11... | collective-permute-start | bytes 5505032 | tf_op jit(solution)/shard_map/ppermute | solution.py:13
  54.8 18.6 %collective-permute-start.1 = (bf16[128,7168]{1,0:T(8,128)(2,1)}, bf16[128,7168]{1,0:T(8,128)(2,1)}, u32[]{:S(2)}, u32[]{:S(2)}) collective-permute-start(bf16[128,7168]{1,0:T(8,128)(2,1)} %slice.82), channel_id=1, source_target_pairs={{0,1},{1,0},{2,3},{3,2},{4,5},{5,4},{6,7},{7,6},{8,9},{9,8},{10,11... | collective-permute-start | bytes 5505032 | tf_op jit(solution)/shard_map/ppermute | solution.py:13
  69.3 4.1 %copy-start.6 = (bf16[256,7168]{1,0:T(8,128)(2,1)S(1)}, bf16[256,7168]{1,0:T(8,128)(2,1)}, u32[]{:S(2)}) copy-start(bf16[256,7168]{1,0:T(8,128)(2,1)} %copy-done.5) | copy-start | bytes 11010052
  69.5 8.4 %collective-permute-start.3 = (bf16[128,7168]{1,0:T(8,128)(2,1)S(1)}, bf16[128,7168]{1,0:T(8,128)(2,1)S(1)}, u32[]{:S(2)}, u32[]{:S(2)}) collective-permute-start(bf16[128,7168]{1,0:T(8,128)(2,1)S(1)} %slice.86), channel_id=1, source_target_pairs={{0,1},{1,0},{2,3},{3,2},{4,5},{5,4},{6,7},{7,6},{8,9},{9,8},{10,11... | collective-permute-start | bytes 5505032 | tf_op jit(solution)/shard_map/ppermute | solution.py:13
  75.4 43.2 %collective-permute-start.2 = (bf16[128,7168]{1,0:T(8,128)(2,1)S(1)}, bf16[128,7168]{1,0:T(8,128)(2,1)S(1)}, u32[]{:S(2)}, u32[]{:S(2)}) collective-permute-start(bf16[128,7168]{1,0:T(8,128)(2,1)S(1)} %fusion.16), channel_id=1, source_target_pairs={{0,2},{2,0},{1,3},{3,1},{4,6},{6,4},{5,7},{7,5},{8,10},{10,8},{9,1... | collective-permute-start | bytes 5505032 | tf_op jit(solution)/shard_map/ppermute | solution.py:13
  77.9 5.0 %copy-start.11 = (bf16[128,7168]{1,0:T(8,128)(2,1)}, bf16[128,7168]{1,0:T(8,128)(2,1)S(1)}, u32[]{:S(2)}) copy-start(bf16[128,7168]{1,0:T(8,128)(2,1)S(1)} %collective-permute-done.3) | copy-start | bytes 5505028
  122.0 19.0 %copy-start.7 = (bf16[128,7168]{1,0:T(8,128)(2,1)}, bf16[128,7168]{1,0:T(8,128)(2,1)S(1)}, u32[]{:S(2)}) copy-start(bf16[128,7168]{1,0:T(8,128)(2,1)S(1)} %multiply_convert_fusion.3) | copy-start | bytes 5505028
  122.0 4.0 collective-permute-start.6
  122.0 65.2 %copy-start.12 = (bf16[128,7168]{1,0:T(8,128)(2,1)S(1)}, bf16[128,7168]{1,0:T(8,128)(2,1)}, u32[]{:S(2)}) copy-start(bf16[128,7168]{1,0:T(8,128)(2,1)} %copy-done.11) | copy-start | bytes 5505028
  122.1 69.5 %collective-permute-start.23 = (bf16[256,2048]{1,0:T(8,128)(2,1)}, bf16[256,2048]{1,0:T(8,128)(2,1)}, u32[]{:S(2)}, u32[]{:S(2)}) collective-permute-start(bf16[256,2048]{1,0:T(8,128)(2,1)} %bitcast), channel_id=1, source_target_pairs={{0,2},{2,0},{1,3},{3,1},{4,6},{6,4},{5,7},{7,5},{8,10},{10,8},{9,1... | collective-permute-start | bytes 3145736 | tf_op jit(solution)/shard_map/ppermute | solution.py:13
  123.9 63.4 %collective-permute-start.11 = (bf16[128,7168]{1,0:T(8,128)(2,1)}, bf16[128,7168]{1,0:T(8,128)(2,1)}, u32[]{:S(2)}, u32[]{:S(2)}) collective-permute-start(bf16[128,7168]{1,0:T(8,128)(2,1)} %fusion.17), channel_id=1, source_target_pairs={{0,2},{2,0},{1,3},{3,1},{4,6},{6,4},{5,7},{7,5},{8,10},{10,8},{9,1... | collective-permute-start | bytes 5505032 | tf_op jit(solution)/shard_map/ppermute | solution.py:13
  191.5 42.8 %collective-permute-start.12 = (bf16[128,7168]{1,0:T(8,128)(2,1)}, bf16[128,7168]{1,0:T(8,128)(2,1)}, u32[]{:S(2)}, u32[]{:S(2)}) collective-permute-start(bf16[128,7168]{1,0:T(8,128)(2,1)} %multiply_convert_fusion.2), channel_id=1, source_target_pairs={{0,1},{1,0},{2,3},{3,2},{4,5},{5,4},{6,7},{7,6},{8,9},{9,8},{10,11... | collective-permute-start | bytes 5505032 | tf_op jit(solution)/shard_map/ppermute | solution.py:13
  195.1 11.2 %collective-permute-start.24 = (f32[128,512]{1,0:T(8,128)S(1)}, f32[128,512]{1,0:T(8,128)S(1)}, u32[]{:S(2)}, u32[]{:S(2)}) collective-permute-start(f32[128,512]{1,0:T(8,128)S(1)} %get-tuple-element.76), channel_id=1, source_target_pairs={{0,4},{4,8},{8,12},{12,0},{1,5},{5,9},{9,13},{13,1},{2,6},{6,10},{... | collective-permute-start | bytes 786440 | tf_op jit(solution)/shard_map/ppermute | solution.py:13
  196.9 20.3 %collective-permute-start.25 = (f32[128,512]{1,0:T(8,128)S(1)}, f32[128,512]{1,0:T(8,128)S(1)}, u32[]{:S(2)}, u32[]{:S(2)}) collective-permute-start(f32[128,512]{1,0:T(8,128)S(1)} %get-tuple-element.78), channel_id=1, source_target_pairs={{0,8},{4,12},{8,0},{12,4},{1,9},{5,13},{9,1},{13,5},{2,10},{6,14},... | collective-permute-start | bytes 786440 | tf_op jit(solution)/shard_map/ppermute | solution.py:13
  199.5 17.8 %collective-permute-start.26 = (f32[128,512]{1,0:T(8,128)S(1)}, f32[128,512]{1,0:T(8,128)S(1)}, u32[]{:S(2)}, u32[]{:S(2)}) collective-permute-start(f32[128,512]{1,0:T(8,128)S(1)} %get-tuple-element.77), channel_id=1, source_target_pairs={{0,12},{4,0},{8,4},{12,8},{1,13},{5,1},{9,5},{13,9},{2,14},{6,2},{... | collective-permute-start | bytes 786440 | tf_op jit(solution)/shard_map/ppermute | solution.py:13
  217.4 5.4 %collective-permute-start.33 = (f32[128,256]{1,0:T(8,128)S(1)}, f32[128,256]{1,0:T(8,128)S(1)}, u32[]{:S(2)}, u32[]{:S(2)}) collective-permute-start(f32[128,256]{1,0:T(8,128)S(1)} %get-tuple-element.50), channel_id=1, source_target_pairs={{0,2},{2,0},{1,3},{3,1},{4,6},{6,4},{5,7},{7,5},{8,10},{10,8},{9,1... | collective-permute-start | bytes 393224 | tf_op jit(solution)/shard_map/ppermute | solution.py:13
  222.9 10.8 %collective-permute-start.34 = (f32[128,256]{1,0:T(8,128)S(1)}, f32[128,256]{1,0:T(8,128)S(1)}, u32[]{:S(2)}, u32[]{:S(2)}) collective-permute-start(f32[128,256]{1,0:T(8,128)S(1)} %add.355), channel_id=1, source_target_pairs={{0,12},{4,0},{8,4},{12,8},{1,13},{5,1},{9,5},{13,9},{2,14},{6,2},{... | collective-permute-start | bytes 393224 | tf_op jit(solution)/shard_map/ppermute | solution.py:13
  229.7 40.7 %collective-permute-start.17 = (bf16[128,7168]{1,0:T(8,128)(2,1)}, bf16[128,7168]{1,0:T(8,128)(2,1)}, u32[]{:S(2)}, u32[]{:S(2)}) collective-permute-start(bf16[128,7168]{1,0:T(8,128)(2,1)} %fusion.18), channel_id=1, source_target_pairs={{0,2},{2,0},{1,3},{3,1},{4,6},{6,4},{5,7},{7,5},{8,10},{10,8},{9,1... | collective-permute-start | bytes 5505032 | tf_op jit(solution)/shard_map/ppermute | solution.py:13
  231.2 43.0 %collective-permute-start.35 = (f32[128,256]{1,0:T(8,128)S(1)}, f32[128,256]{1,0:T(8,128)S(1)}, u32[]{:S(2)}, u32[]{:S(2)}) collective-permute-start(f32[128,256]{1,0:T(8,128)S(1)} %add.355), channel_id=1, source_target_pairs={{0,8},{4,12},{8,0},{12,4},{1,9},{5,13},{9,1},{13,5},{2,10},{6,14},... | collective-permute-start | bytes 393224 | tf_op jit(solution)/shard_map/ppermute | solution.py:13
  232.0 42.2 %collective-permute-start.36 = (f32[128,256]{1,0:T(8,128)S(1)}, f32[128,256]{1,0:T(8,128)S(1)}, u32[]{:S(2)}, u32[]{:S(2)}) collective-permute-start(f32[128,256]{1,0:T(8,128)S(1)} %add.355), channel_id=1, source_target_pairs={{0,4},{4,8},{8,12},{12,0},{1,5},{5,9},{9,13},{13,1},{2,6},{6,10},{... | collective-permute-start | bytes 393224 | tf_op jit(solution)/shard_map/ppermute | solution.py:13
  234.3 36.2 %copy-start.4 = (bf16[256,7168]{1,0:T(8,128)(2,1)S(1)}, bf16[256,7168]{1,0:T(8,128)(2,1)}, u32[]{:S(2)}) copy-start(bf16[256,7168]{1,0:T(8,128)(2,1)} %copy-done.3) | copy-start | bytes 11010052
  250.0 24.2 %copy-start.17 = (f32[1024,256]{1,0:T(8,128)S(1)}, f32[1024,256]{1,0:T(8,128)}, u32[]{:S(2)}) copy-start(f32[1024,256]{1,0:T(8,128)} %constant_dynamic-update-slice_fusion.7) | copy-start | bytes 3145732
  250.0 25.3 %copy-start = (bf16[8,32,7168]{2,1,0:T(8,128)(2,1)S(1)}, bf16[8,32,7168]{2,1,0:T(8,128)(2,1)}, u32[]{:S(2)}) copy-start(bf16[8,32,7168]{2,1,0:T(8,128)(2,1)} %param.10) | copy-start | bytes 11010052
  250.0 25.3 %copy-start.8 = (bf16[128,7168]{1,0:T(8,128)(2,1)S(1)}, bf16[128,7168]{1,0:T(8,128)(2,1)}, u32[]{:S(2)}) copy-start(bf16[128,7168]{1,0:T(8,128)(2,1)} %copy-done.7) | copy-start | bytes 5505028
  274.1 36.2 %collective-permute-start.18 = (bf16[128,7168]{1,0:T(8,128)(2,1)S(1)}, bf16[128,7168]{1,0:T(8,128)(2,1)S(1)}, u32[]{:S(2)}, u32[]{:S(2)}) collective-permute-start(bf16[128,7168]{1,0:T(8,128)(2,1)S(1)} %multiply_convert_fusion.1), channel_id=1, source_target_pairs={{0,1},{1,0},{2,3},{3,2},{4,5},{5,4},{6,7},{7,6},{8,9},{9,8},{10,11... | collective-permute-start | bytes 5505032 | tf_op jit(solution)/shard_map/ppermute | solution.py:13
  276.7 28.9 %copy-start.14 = (bf16[256,2048]{1,0:T(8,128)(2,1)S(1)}, bf16[256,2048]{1,0:T(8,128)(2,1)}, u32[]{:S(2)}) copy-start(bf16[256,2048]{1,0:T(8,128)(2,1)} %fusion.26) | copy-start | bytes 3145732
  276.8 11.9 %collective-permute-start.10 = (bf16[128,1024]{1,0:T(8,128)(2,1)S(1)}, bf16[128,1024]{1,0:T(8,128)(2,1)S(1)}, u32[]{:S(2)}, u32[]{:S(2)}) collective-permute-start(bf16[128,1024]{1,0:T(8,128)(2,1)S(1)} %get-tuple-element.60), channel_id=1, source_target_pairs={{0,5},{1,13},{4,0},{5,8},{8,1},{9,9},{12,4},{13,12},{2,7},{3,15},{... | collective-permute-start | bytes 786440 | tf_op jit(solution)/shard_map/ppermute | solution.py:85
  279.3 11.0 %collective-permute-start.7 = (bf16[128,1024]{1,0:T(8,128)(2,1)S(1)}, bf16[128,1024]{1,0:T(8,128)(2,1)S(1)}, u32[]{:S(2)}, u32[]{:S(2)}) collective-permute-start(bf16[128,1024]{1,0:T(8,128)(2,1)S(1)} %get-tuple-element.63), channel_id=1, source_target_pairs={{0,0},{1,8},{4,1},{5,9},{8,4},{9,12},{12,5},{13,13},{2,2},{3,10},{... | collective-permute-start | bytes 786440 | tf_op jit(solution)/shard_map/ppermute | solution.py:85
  280.0 15.0 %collective-permute-start.8 = (bf16[128,1024]{1,0:T(8,128)(2,1)S(1)}, bf16[128,1024]{1,0:T(8,128)(2,1)S(1)}, u32[]{:S(2)}, u32[]{:S(2)}) collective-permute-start(bf16[128,1024]{1,0:T(8,128)(2,1)S(1)} %get-tuple-element.62), channel_id=1, source_target_pairs={{0,1},{1,9},{4,4},{5,12},{8,5},{9,13},{12,0},{13,8},{2,3},{3,11},{... | collective-permute-start | bytes 786440 | tf_op jit(solution)/shard_map/ppermute | solution.py:85
  285.8 19.8 %collective-permute-start.9 = (bf16[128,1024]{1,0:T(8,128)(2,1)S(1)}, bf16[128,1024]{1,0:T(8,128)(2,1)S(1)}, u32[]{:S(2)}, u32[]{:S(2)}) collective-permute-start(bf16[128,1024]{1,0:T(8,128)(2,1)S(1)} %get-tuple-element.61), channel_id=1, source_target_pairs={{0,4},{1,12},{4,5},{5,13},{8,0},{9,8},{12,1},{13,9},{2,6},{3,14},{... | collective-permute-start | bytes 786440 | tf_op jit(solution)/shard_map/ppermute | solution.py:85
  288.8 21.5 %copy-start.20 = (bf16[128,1024]{1,0:T(8,128)(2,1)}, bf16[128,1024]{1,0:T(8,128)(2,1)S(1)}, u32[]{:S(2)}) copy-start(bf16[128,1024]{1,0:T(8,128)(2,1)S(1)} %collective-permute-done.10) | copy-start | bytes 786436
  288.8 41.6 %collective-permute-start.27 = (bf16[128,7168]{1,0:T(8,128)(2,1)}, bf16[128,7168]{1,0:T(8,128)(2,1)}, u32[]{:S(2)}, u32[]{:S(2)}) collective-permute-start(bf16[128,7168]{1,0:T(8,128)(2,1)} %fusion.19), channel_id=1, source_target_pairs={{0,2},{2,0},{1,3},{3,1},{4,6},{6,4},{5,7},{7,5},{8,10},{10,8},{9,1... | collective-permute-start | bytes 5505032 | tf_op jit(solution)/shard_map/ppermute | solution.py:13
  290.3 20.0 %copy-start.22 = (bf16[128,1024]{1,0:T(8,128)(2,1)}, bf16[128,1024]{1,0:T(8,128)(2,1)S(1)}, u32[]{:S(2)}) copy-start(bf16[128,1024]{1,0:T(8,128)(2,1)S(1)} %collective-permute-done.7) | copy-start | bytes 786436
  295.0 15.3 %copy-start.24 = (bf16[128,1024]{1,0:T(8,128)(2,1)}, bf16[128,1024]{1,0:T(8,128)(2,1)S(1)}, u32[]{:S(2)}) copy-start(bf16[128,1024]{1,0:T(8,128)(2,1)S(1)} %collective-permute-done.8) | copy-start | bytes 786436
  305.6 4.7 %copy-start.26 = (bf16[128,1024]{1,0:T(8,128)(2,1)}, bf16[128,1024]{1,0:T(8,128)(2,1)S(1)}, u32[]{:S(2)}) copy-start(bf16[128,1024]{1,0:T(8,128)(2,1)S(1)} %collective-permute-done.9) | copy-start | bytes 786436
  306.7 36.4 %collective-permute-start.13 = (bf16[128,1024]{1,0:T(8,128)(2,1)}, bf16[128,1024]{1,0:T(8,128)(2,1)S(1)}, u32[]{:S(2)}, u32[]{:S(2)}) collective-permute-start(bf16[128,1024]{1,0:T(8,128)(2,1)} %get-tuple-element.67), channel_id=1, source_target_pairs={{0,0},{1,8},{4,1},{5,9},{8,4},{9,12},{12,5},{13,13},{2,2},{3,10},{... | collective-permute-start | bytes 786440 | tf_op jit(solution)/shard_map/ppermute | solution.py:85
  308.3 34.9 %collective-permute-start.14 = (bf16[128,1024]{1,0:T(8,128)(2,1)}, bf16[128,1024]{1,0:T(8,128)(2,1)S(1)}, u32[]{:S(2)}, u32[]{:S(2)}) collective-permute-start(bf16[128,1024]{1,0:T(8,128)(2,1)} %get-tuple-element.66), channel_id=1, source_target_pairs={{0,1},{1,9},{4,4},{5,12},{8,5},{9,13},{12,0},{13,8},{2,3},{3,11},{... | collective-permute-start | bytes 786440 | tf_op jit(solution)/shard_map/ppermute | solution.py:85
  310.2 33.0 %collective-permute-start.15 = (bf16[128,1024]{1,0:T(8,128)(2,1)}, bf16[128,1024]{1,0:T(8,128)(2,1)}, u32[]{:S(2)}, u32[]{:S(2)}) collective-permute-start(bf16[128,1024]{1,0:T(8,128)(2,1)} %get-tuple-element.65), channel_id=1, source_target_pairs={{0,4},{1,12},{4,5},{5,13},{8,0},{9,8},{12,1},{13,9},{2,6},{3,14},{... | collective-permute-start | bytes 786440 | tf_op jit(solution)/shard_map/ppermute | solution.py:85
  311.6 18.7 %copy-start.2 = (bf16[256,7168]{1,0:T(8,128)(2,1)S(1)}, bf16[256,7168]{1,0:T(8,128)(2,1)}, u32[]{:S(2)}) copy-start(bf16[256,7168]{1,0:T(8,128)(2,1)} %copy-done.1) | copy-start | bytes 11010052
  311.6 31.6 %collective-permute-start.16 = (bf16[128,1024]{1,0:T(8,128)(2,1)}, bf16[128,1024]{1,0:T(8,128)(2,1)}, u32[]{:S(2)}, u32[]{:S(2)}) collective-permute-start(bf16[128,1024]{1,0:T(8,128)(2,1)} %get-tuple-element.64), channel_id=1, source_target_pairs={{0,5},{1,13},{4,0},{5,8},{8,1},{9,9},{12,4},{13,12},{2,7},{3,15},{... | collective-permute-start | bytes 786440 | tf_op jit(solution)/shard_map/ppermute | solution.py:85
  330.3 7.4 %copy-start.21 = (bf16[128,1024]{1,0:T(8,128)(2,1)S(1)}, bf16[128,1024]{1,0:T(8,128)(2,1)}, u32[]{:S(2)}) copy-start(bf16[128,1024]{1,0:T(8,128)(2,1)} %copy-done.20) | copy-start | bytes 786436
  330.3 7.4 %copy-start.23 = (bf16[128,1024]{1,0:T(8,128)(2,1)S(1)}, bf16[128,1024]{1,0:T(8,128)(2,1)}, u32[]{:S(2)}) copy-start(bf16[128,1024]{1,0:T(8,128)(2,1)} %copy-done.22) | copy-start | bytes 786436
  330.3 7.4 %copy-start.25 = (bf16[128,1024]{1,0:T(8,128)(2,1)S(1)}, bf16[128,1024]{1,0:T(8,128)(2,1)}, u32[]{:S(2)}) copy-start(bf16[128,1024]{1,0:T(8,128)(2,1)} %copy-done.24) | copy-start | bytes 786436
  330.3 7.4 %copy-start.27 = (bf16[128,1024]{1,0:T(8,128)(2,1)S(1)}, bf16[128,1024]{1,0:T(8,128)(2,1)}, u32[]{:S(2)}) copy-start(bf16[128,1024]{1,0:T(8,128)(2,1)} %copy-done.26) | copy-start | bytes 786436
  330.3 7.5 %copy-start.10 = (bf16[128,7168]{1,0:T(8,128)(2,1)S(1)}, bf16[128,7168]{1,0:T(8,128)(2,1)}, u32[]{:S(2)}) copy-start(bf16[128,7168]{1,0:T(8,128)(2,1)} %copy-done.9) | copy-start | bytes 5505028
  335.1 18.4 %collective-permute-start.28 = (bf16[128,7168]{1,0:T(8,128)(2,1)}, bf16[128,7168]{1,0:T(8,128)(2,1)}, u32[]{:S(2)}, u32[]{:S(2)}) collective-permute-start(bf16[128,7168]{1,0:T(8,128)(2,1)} %multiply_convert_fusion), channel_id=1, source_target_pairs={{0,1},{1,0},{2,3},{3,2},{4,5},{5,4},{6,7},{7,6},{8,9},{9,8},{10,11... | collective-permute-start | bytes 5505032 | tf_op jit(solution)/shard_map/ppermute | solution.py:13
  339.3 3.4 copy-start.28
  339.3 3.5 copy-start.15
  343.1 7.1 %collective-permute-start.37 = (f32[16,8]{0,1:T(8,128)S(1)}, f32[16,8]{0,1:T(8,128)S(1)}, u32[]{:S(2)}, u32[]{:S(2)}) collective-permute-start(f32[16,8]{0,1:T(8,128)S(1)} %convolution_multiply_fusion), channel_id=1, source_target_pairs={{0,1},{1,0},{2,3},{3,2},{4,5},{5,4},{6,7},{7,6},{8,9},{9,8},{10,11... | collective-permute-start | bytes 1544 | tf_op jit(solution)/shard_map/ppermute | solution.py:13
  343.2 25.7 %collective-permute-start.19 = (bf16[128,1024]{1,0:T(8,128)(2,1)S(1)}, bf16[128,1024]{1,0:T(8,128)(2,1)S(1)}, u32[]{:S(2)}, u32[]{:S(2)}) collective-permute-start(bf16[128,1024]{1,0:T(8,128)(2,1)S(1)} %get-tuple-element.71), channel_id=1, source_target_pairs={{0,0},{1,8},{4,1},{5,9},{8,4},{9,12},{12,5},{13,13},{2,2},{3,10},{... | collective-permute-start | bytes 786440 | tf_op jit(solution)/shard_map/ppermute | solution.py:85
  343.9 26.8 %collective-permute-start.20 = (bf16[128,1024]{1,0:T(8,128)(2,1)S(1)}, bf16[128,1024]{1,0:T(8,128)(2,1)S(1)}, u32[]{:S(2)}, u32[]{:S(2)}) collective-permute-start(bf16[128,1024]{1,0:T(8,128)(2,1)S(1)} %get-tuple-element.70), channel_id=1, source_target_pairs={{0,1},{1,9},{4,4},{5,12},{8,5},{9,13},{12,0},{13,8},{2,3},{3,11},{... | collective-permute-start | bytes 786440 | tf_op jit(solution)/shard_map/ppermute | solution.py:85
  350.1 22.4 %collective-permute-start.21 = (bf16[128,1024]{1,0:T(8,128)(2,1)S(1)}, bf16[128,1024]{1,0:T(8,128)(2,1)S(1)}, u32[]{:S(2)}, u32[]{:S(2)}) collective-permute-start(bf16[128,1024]{1,0:T(8,128)(2,1)S(1)} %get-tuple-element.69), channel_id=1, source_target_pairs={{0,4},{1,12},{4,5},{5,13},{8,0},{9,8},{12,1},{13,9},{2,6},{3,14},{... | collective-permute-start | bytes 786440 | tf_op jit(solution)/shard_map/ppermute | solution.py:85
  350.2 22.3 %collective-permute-start.22 = (bf16[128,1024]{1,0:T(8,128)(2,1)S(1)}, bf16[128,1024]{1,0:T(8,128)(2,1)S(1)}, u32[]{:S(2)}, u32[]{:S(2)}) collective-permute-start(bf16[128,1024]{1,0:T(8,128)(2,1)S(1)} %get-tuple-element.68), channel_id=1, source_target_pairs={{0,5},{1,13},{4,0},{5,8},{8,1},{9,9},{12,4},{13,12},{2,7},{3,15},{... | collective-permute-start | bytes 786440 | tf_op jit(solution)/shard_map/ppermute | solution.py:85
  367.8 10.0 %collective-permute-start.38 = (f32[16,8]{0,1:T(8,128)S(1)}, f32[16,8]{0,1:T(8,128)S(1)}, u32[]{:S(2)}, u32[]{:S(2)}) collective-permute-start(f32[16,8]{0,1:T(8,128)S(1)} %add.357), channel_id=1, source_target_pairs={{0,4},{4,8},{8,12},{12,0},{1,5},{5,9},{9,13},{13,1},{2,6},{6,10},{... | collective-permute-start | bytes 1544 | tf_op jit(solution)/shard_map/ppermute | solution.py:13
  368.9 9.0 %collective-permute-start.39 = (f32[16,8]{0,1:T(8,128)S(1)}, f32[16,8]{0,1:T(8,128)S(1)}, u32[]{:S(2)}, u32[]{:S(2)}) collective-permute-start(f32[16,8]{0,1:T(8,128)S(1)} %add.357), channel_id=1, source_target_pairs={{0,8},{4,12},{8,0},{12,4},{1,9},{5,13},{9,1},{13,5},{2,10},{6,14},... | collective-permute-start | bytes 1544 | tf_op jit(solution)/shard_map/ppermute | solution.py:13
  370.6 12.2 %collective-permute-start.40 = (f32[16,8]{0,1:T(8,128)S(1)}, f32[16,8]{0,1:T(8,128)S(1)}, u32[]{:S(2)}, u32[]{:S(2)}) collective-permute-start(f32[16,8]{0,1:T(8,128)S(1)} %add.357), channel_id=1, source_target_pairs={{0,12},{4,0},{8,4},{12,8},{1,13},{5,1},{9,5},{13,9},{2,14},{6,2},{... | collective-permute-start | bytes 1544 | tf_op jit(solution)/shard_map/ppermute | solution.py:13
  372.5 10.9 %collective-permute-start.29 = (bf16[128,1024]{1,0:T(8,128)(2,1)S(1)}, bf16[128,1024]{1,0:T(8,128)(2,1)S(1)}, u32[]{:S(2)}, u32[]{:S(2)}) collective-permute-start(bf16[128,1024]{1,0:T(8,128)(2,1)S(1)} %get-tuple-element.72), channel_id=1, source_target_pairs={{0,0},{1,8},{4,1},{5,9},{8,4},{9,12},{12,5},{13,13},{2,2},{3,10},{... | collective-permute-start | bytes 786440 | tf_op jit(solution)/shard_map/ppermute | solution.py:85
  373.2 13.2 %collective-permute-start.30 = (bf16[128,1024]{1,0:T(8,128)(2,1)S(1)}, bf16[128,1024]{1,0:T(8,128)(2,1)S(1)}, u32[]{:S(2)}, u32[]{:S(2)}) collective-permute-start(bf16[128,1024]{1,0:T(8,128)(2,1)S(1)} %get-tuple-element.75), channel_id=1, source_target_pairs={{0,1},{1,9},{4,4},{5,12},{8,5},{9,13},{12,0},{13,8},{2,3},{3,11},{... | collective-permute-start | bytes 786440 | tf_op jit(solution)/shard_map/ppermute | solution.py:85
  377.8 19.4 %collective-permute-start.31 = (bf16[128,1024]{1,0:T(8,128)(2,1)S(1)}, bf16[128,1024]{1,0:T(8,128)(2,1)S(1)}, u32[]{:S(2)}, u32[]{:S(2)}) collective-permute-start(bf16[128,1024]{1,0:T(8,128)(2,1)S(1)} %get-tuple-element.74), channel_id=1, source_target_pairs={{0,4},{1,12},{4,5},{5,13},{8,0},{9,8},{12,1},{13,9},{2,6},{3,14},{... | collective-permute-start | bytes 786440 | tf_op jit(solution)/shard_map/ppermute | solution.py:85
  377.9 19.3 %collective-permute-start.32 = (bf16[128,1024]{1,0:T(8,128)(2,1)S(1)}, bf16[128,1024]{1,0:T(8,128)(2,1)S(1)}, u32[]{:S(2)}, u32[]{:S(2)}) collective-permute-start(bf16[128,1024]{1,0:T(8,128)(2,1)S(1)} %get-tuple-element.73), channel_id=1, source_target_pairs={{0,5},{1,13},{4,0},{5,8},{8,1},{9,9},{12,4},{13,12},{2,7},{3,15},{... | collective-permute-start | bytes 786440 | tf_op jit(solution)/shard_map/ppermute | solution.py:85
  (8 other events, 15.3 us)
